TPU v7x, 256 devices: a whole 4x4x8 slice. The times are simulated.
256 devices in a mesh: dap: 128 (over y, x, z_hi, core), dp: 2 (over z_lo).
Axes of the slice: x: 4, y: 4, z: 8 (z_hi: 4, z_lo: 2; z = z_hi * 2 + z_lo), core: 2. Of those that a mesh axis runs over, the one named last changes fastest.
Arguments:
- pair: bfloat16 [512, 256, 128], P(('dp', 'dap')), parts along dimension 0
- token_mask: int32 [512], P('dp'), parts along dimension 0, may hold values from 0 to 1, as said below
- chain_ids: int32 [512], P('dp'), parts along dimension 0, may hold values from 0 to 3, never falling along the last dimension, each value on 1 to 128 neighbouring positions
- proj_weight: bfloat16 [128, 512], replicated
- bias_weight: bfloat16 [128, 4], replicated, may hold values from -0.5 to 0.5
- chain_weight: float32 [4], replicated, may hold values from -1.5 to 1.5
- out_weight: bfloat16 [128, 128], replicated, may hold values from -0.5 to 0.5
- cotangent: bfloat16 [512, 256, 128], P(('dp', 'dap')), parts along dimension 0, may hold values from -24 to 24
Outputs:
- next_pair_t: float32 [512, 256, 128], P(('dp', 'dap')), parts along dimension 0
- pair_grad: bfloat16 [512, 256, 128], P(('dp', 'dap')), parts along dimension 0
- proj_grad: float32 [256, 512], P('dp'), parts along dimension 0
- bias_weight_grad: float32 [256, 4], P('dp'), parts along dimension 0
- chain_grad: float32 [8], P('dp'), parts along dimension 0
- out_grad: float32 [256, 128], P('dp'), parts along dimension 0
There are 2 independent parts, one for each index of `dp`. A program takes and returns all parts, laid end to end along the dimension named above; an argument that names none is the same for every part. Nothing has to cross between parts.
Inputs may be any that keep to these rules, and one draw needn't show every extreme that they name: `token_mask`: tokens are real up to some point and padding after it; the first 128 tokens are real and the last token is padding. `chain_ids`: chain numbers never fall along the tokens; every chain has 1 to 128 tokens, one chain exactly 128.
All inputs are finite; a program needn't handle non-finite values.
Results may differ from a plain program's by a relative error of at most 0.011.
Values may be sent and summed in bfloat16 or wider, within the bound.
A program may use at most 64 MiB of HBM per device.

v0:
```python
import jax
import jax.numpy as jnp
from jax import lax
from jax.sharding import PartitionSpec as P

H = 4
DH = 32
HD = 128
epsilon = 1e-05
contract_rows = (((0,), (0,)), ((), ()))
contract_cols = (((1,), (1,)), ((), ()))


def normalize(pair):
    values_f = pair.astype(jnp.float32)
    centered = values_f - jnp.mean(values_f, axis=-1, keepdims=True)
    inverse = lax.rsqrt(jnp.mean(centered * centered, axis=-1, keepdims=True) + epsilon)
    return (centered * inverse, inverse)


def row_softmax(query_row, key_row, bias_head, extra_head):
    scores = lax.dot_general(query_row, key_row, contract_cols, preferred_element_type=jnp.float32)
    scores = scores + bias_head.astype(jnp.float32) + extra_head
    highest = jnp.max(scores, axis=1, keepdims=True)
    expo_s = jnp.exp(scores - highest)
    return expo_s / jnp.sum(expo_s, axis=1, keepdims=True)


def forward_rows(query_h, key_h, value_h, bias_head, extra_head):

    def forward_one_row(items):
        query_row, key_row, value_row = items
        attention = row_softmax(query_row, key_row, bias_head, extra_head)
        return jnp.dot(
            attention.astype(jnp.bfloat16), value_row, preferred_element_type=jnp.float32
        )

    return lax.map(forward_one_row, (query_h, key_h, value_h))


def backward_rows(query_h, key_h, value_h, grad_h, bias_head, extra_head):

    def backward_one_row(summed, items):
        query_row, key_row, value_row, grad_row = items
        attention = row_softmax(query_row, key_row, bias_head, extra_head)
        d_probs = lax.dot_general(
            grad_row, value_row, contract_cols, preferred_element_type=jnp.float32
        )
        inner_sum = jnp.sum(attention * d_probs, axis=1, keepdims=True)
        d_scores = attention * (d_probs - inner_sum)
        scores_low = d_scores.astype(jnp.bfloat16)
        d_query = jnp.dot(scores_low, key_row, preferred_element_type=jnp.float32)
        d_key = lax.dot_general(
            scores_low, query_row, contract_rows, preferred_element_type=jnp.float32
        )
        d_value = lax.dot_general(
            attention.astype(jnp.bfloat16),
            grad_row,
            contract_rows,
            preferred_element_type=jnp.float32,
        )
        return (summed + d_scores, (d_query, d_key, d_value))

    tokens = bias_head.shape[1]
    return lax.scan(
        backward_one_row,
        jnp.zeros((tokens, tokens), jnp.float32),
        (query_h, key_h, value_h, grad_h),
    )


def body(
    pair, token_mask, chain_ids, proj_weight, bias_weight, chain_weight, out_weight, cotangent
):
    row_count, length, channels = pair.shape
    standard, inverse = normalize(pair)
    normed = standard.astype(jnp.bfloat16)
    flat_x = normed.reshape(row_count * length, channels)
    projected = jnp.dot(flat_x, proj_weight, preferred_element_type=jnp.float32).reshape(
        row_count, length, 4 * HD
    )
    scaling = DH ** (-0.5)
    query = (projected[..., :HD] * scaling).astype(jnp.bfloat16)
    key_rows = projected[..., HD : 2 * HD].astype(jnp.bfloat16)
    value_rows = projected[..., 2 * HD : 3 * HD].astype(jnp.bfloat16)
    gating = jax.nn.sigmoid(projected[..., 3 * HD :])
    local_bias = jnp.dot(flat_x, bias_weight, preferred_element_type=jnp.float32).reshape(
        row_count, length, H
    )
    local_bias = jnp.transpose(local_bias, (2, 0, 1)).astype(jnp.bfloat16)
    pair_bias = lax.all_gather(local_bias, "dap", axis=1, tiled=True)
    same_chain = (chain_ids[:, None] == chain_ids[None, :]).astype(jnp.float32)
    masked = (token_mask.astype(jnp.float32) - 1.0) * 1000000000.0
    outputs = []
    for number in range(H):
        columns = slice(number * DH, (number + 1) * DH)
        extra_head = chain_weight[number] * same_chain + masked[None, :]
        outputs.append(
            forward_rows(
                query[:, :, columns],
                key_rows[:, :, columns],
                value_rows[:, :, columns],
                pair_bias[number],
                extra_head,
            )
        )
    attended = jnp.concatenate(outputs, axis=-1)
    gated = (gating * attended).astype(jnp.bfloat16)
    gated_flat = gated.reshape(row_count * length, HD)
    update = jnp.dot(gated_flat, out_weight, preferred_element_type=jnp.float32).reshape(
        row_count, length, channels
    )
    next_pair = pair.astype(jnp.float32) + update
    next_pair_t = lax.all_to_all(
        jnp.transpose(next_pair, (1, 0, 2)), "dap", split_axis=0, concat_axis=1, tiled=True
    )
    grad_flat = cotangent.reshape(row_count * length, channels)
    out_part = (
        lax.dot_general(gated_flat, grad_flat, contract_rows, preferred_element_type=jnp.float32)
        / length
    )
    d_gated = lax.dot_general(
        grad_flat, out_weight, contract_cols, preferred_element_type=jnp.float32
    ).reshape(row_count, length, HD)
    d_attended = (d_gated * gating).astype(jnp.bfloat16)
    d_gate = d_gated * attended * gating * (1.0 - gating)
    query_parts, key_parts, value_parts, totals, shares = ([], [], [], [], [])
    for number in range(H):
        columns = slice(number * DH, (number + 1) * DH)
        extra_head = chain_weight[number] * same_chain + masked[None, :]
        summed, (d_query, d_key, d_value) = backward_rows(
            query[:, :, columns],
            key_rows[:, :, columns],
            value_rows[:, :, columns],
            d_attended[:, :, columns],
            pair_bias[number],
            extra_head,
        )
        query_parts.append(d_query)
        key_parts.append(d_key)
        value_parts.append(d_value)
        totals.append(summed)
    spread = lax.psum_scatter(jnp.stack(totals, axis=0), "dap", scatter_dimension=1, tiled=True)
    bias_total = jnp.transpose(spread, (1, 2, 0))
    d_proj = jnp.concatenate(
        [
            jnp.concatenate(query_parts, axis=-1) * scaling,
            jnp.concatenate(key_parts, axis=-1),
            jnp.concatenate(value_parts, axis=-1),
            d_gate,
        ],
        axis=-1,
    ).astype(jnp.bfloat16)
    d_bias = bias_total.astype(jnp.bfloat16)
    d_proj_flat = d_proj.reshape(row_count * length, 4 * HD)
    d_bias_flat = d_bias.reshape(row_count * length, H)
    d_normed = lax.dot_general(
        d_proj_flat, proj_weight, contract_cols, preferred_element_type=jnp.float32
    )
    d_normed = d_normed + lax.dot_general(
        d_bias_flat, bias_weight, contract_cols, preferred_element_type=jnp.float32
    )
    d_normed = d_normed.reshape(row_count, length, channels)
    mean_grad = jnp.mean(d_normed, axis=-1, keepdims=True)
    mean_cross = jnp.mean(d_normed * standard, axis=-1, keepdims=True)
    pair_grad = ((d_normed - mean_grad - standard * mean_cross) * inverse).astype(jnp.bfloat16)
    proj_part = (
        lax.dot_general(flat_x, d_proj_flat, contract_rows, preferred_element_type=jnp.float32)
        / length
    )
    biasw_part = (
        lax.dot_general(flat_x, d_bias_flat, contract_rows, preferred_element_type=jnp.float32)
        / length
    )
    start_row = lax.axis_index("dap") * row_count
    local_chain = lax.dynamic_slice_in_dim(chain_ids, start_row, row_count)
    same_local = (local_chain[:, None] == chain_ids[None, :]).astype(jnp.float32)
    chain_part = jnp.sum(bias_total * same_local[:, :, None], axis=(0, 1)) / length
    proj_grad, bias_weight_grad, chain_grad, out_grad = lax.psum(
        (proj_part, biasw_part, chain_part, out_part), "dap"
    )
    return (next_pair_t, pair_grad, proj_grad, bias_weight_grad, chain_grad, out_grad)


def solution(mesh):
    return jax.shard_map(
        body,
        mesh=mesh,
        in_specs=(
            P(("dp", "dap"), None, None),
            P("dp"),
            P("dp"),
            P(),
            P(),
            P(),
            P(),
            P(("dp", "dap"), None, None),
        ),
        out_specs=(
            P(("dp", "dap"), None, None),
            P(("dp", "dap"), None, None),
            P("dp", None),
            P("dp", None),
            P("dp"),
            P("dp", None),
        ),
        check_vma=False,
    )
```

profile of v0, /device:TPU:32, one launch (start us, length us, event | category | flops | bytes accessed | tf_op | source)
XLA Modules:
  0.0 1958.6 jit_solution(10141085470042809085)
XLA Ops:
  7.2 1.1 convert_reduce_fusion
  9.9 195.9 %all_gather.3 = bf16[4,256,256]{2,0,1:T(4,128)(2,1)S(1)} all-gather(bf16[4,2,256]{2,0,1:T(4,128)(2,1)S(1)} %fusion.179), channel_id=1, replica_groups=mesh['dap'=128,'dp'=2] {'dap'}, dimensions={1}, use_global_device_ids=true | all-gather | bytes 528384 | tf_op jit(solution)/shard_map/all_gather | solution.py:91
  205.8 1.4 fusion.218
  209.3 1.2 fusion.217
  211.1 5.6 while.115
  211.1 1.7 fusion.320
  212.9 0.8 copy-done.27
  213.9 1.7 fusion.320
  218.5 5.7 while.114
  218.5 1.8 fusion.316
  221.3 1.8 fusion.316
  224.2 0.8 copy.98
  226.0 3.6 while.113
  226.0 1.5 fusion.312
  227.8 1.5 fusion.312
  231.1 3.7 while.112
  231.1 1.6 fusion.308
  233.0 1.5 fusion.308
  235.5 0.8 copy.96
  236.3 1.9 multiply_convert_fusion
  238.5 0.9 copy.100
  239.4 6.2 all-to-all-start
  249.5 0.8 fusion.178
  250.3 0.9 fusion.219
  251.9 12.2 while.119
  251.9 1.5 fusion.365
  255.2 0.9 fusion.367
  258.0 1.5 fusion.365
  261.3 0.9 fusion.367
  264.9 8.8 while.118
  264.9 1.8 fusion.353
  269.3 1.8 fusion.353
  275.1 8.3 while.117
  275.1 1.6 fusion.341
  276.8 0.8 copy-done.44
  279.3 1.5 fusion.341
  280.9 0.8 copy-done.44
  284.3 6.9 while.116
  284.3 1.5 fusion.329
  287.7 1.6 fusion.329
  294.3 0.8 copy.144
  295.1 0.8 copy.143
  295.9 0.8 copy.142
  299.5 1.1 fusion.176
  300.6 2.0 pad_maximum_fusion
  307.6 1290.5 %all-reduce.5.cloned.1.call-done = (f32[4,256,256]{2,0,1:T(4,128)}, f32[128,512]{1,0:T(8,128)}, f32[128,128]{1,0:T(8,128)}) async-done(((f32[4,256,256]{2,0,1:T(4,128)}, f32[128,512]{1,0:T(8,128)}, f32[128,128]{1,0:T(8,128)}), (f32[4,256,256]{2,0,1:T(4,128)}, f32[128,512]{1,0:T(8,128)}, f32[128,128]{1,0:T(8,128)})) %all-reduce.5.cloned.1.call-update) | async-done | bytes 1376272
  1601.4 1.0 fusion.189
  1602.4 347.9 %all-reduce.1 = (f32[128,4]{0,1:T(4,128)}, f32[4]{0:T(128)}) all-reduce(f32[128,4]{0,1:T(4,128)S(1)} %fusion.180, f32[4]{0:T(128)S(1)} %broadcast_multiply_fusion.3), channel_id=1, replica_groups=mesh['dap'=128,'dp'=2] {'dap'}, use_global_device_ids=true, to_apply=%region_42.43 | all-reduce | flops 516 | bytes 4128 | tf_op jit(solution)/shard_map/psum | solution.py:179
  (296 shorter events, 56.1 us)
Async XLA Ops:
  7.2 1.4 copy-start
  7.2 1.1 copy-start.1
  212.8 0.9 copy-start.27
  215.6 0.9 copy-start.27
  216.7 0.9 copy-start.4
  220.2 0.9 copy-start.22
  223.1 0.9 copy-start.22
  224.2 0.8 copy-start.2
  225.1 0.9 copy-start.18
  230.2 0.9 copy-start.16
  231.1 5.2 copy-start.41
  234.8 1.5 copy-start.56
  234.8 1.5 copy-start.14
  235.5 0.8 copy-start.51
  239.4 67.5 %all-to-all-start = ((f32[256,2,128]{2,1,0:T(2,128)}), f32[256,2,128]{2,1,0:T(2,128)S(1)}, u32[]{:S(2)}, u32[]{:S(2)}) async-start(f32[256,2,128]{2,1,0:T(2,128)} %copy.100), calls=%async_computation | async-start | bytes 524288 | tf_op jit(solution)/shard_map/all_to_all | solution.py:114
  245.6 1352.6 %all-reduce.5.cloned.1.call-start = ((), (), s32[]{:S(2)}) async-start(), calls=%async_computation.1 | async-start | bytes 2752512
  247.0 2.4 copy-start.42
  250.3 0.9 copy-start.26
  251.9 12.8 copy-start.3
  251.9 12.8 copy-start.23
  253.4 0.9 copy-start.28
  253.4 1.0 copy-start.48
  256.2 0.9 copy-start.49
  259.5 0.9 copy-start.28
  259.5 1.0 copy-start.48
  262.3 0.9 copy-start.49
  264.9 10.0 copy-start.19
  264.9 10.0 copy-start.25
  266.7 0.9 copy-start.46
  268.2 0.9 copy-start.47
  271.1 0.9 copy-start.46
  272.6 0.9 copy-start.47
  275.1 8.4 copy-start.17
  275.1 8.4 copy-start.21
  276.7 0.9 copy-start.44
  278.2 0.9 copy-start.45
  280.9 0.9 copy-start.44
  282.4 0.9 copy-start.45
  285.8 0.9 copy-start.43
  289.3 0.9 copy-start.43
  296.9 0.8 copy-start.11
  298.0 0.9 copy-start.12
  299.5 1.1 copy-start.5
  299.5 1.1 copy-start.6
  299.5 1.1 copy-start.7
  303.2 0.9 copy-start.13
  1601.4 348.9 %copy-start.15 = (f32[128,512]{1,0:T(8,128)S(1)}, f32[128,512]{1,0:T(8,128)}, u32[]{:S(2)}) copy-start(f32[128,512]{1,0:T(8,128)} %get-tuple-element.2116) | copy-start | bytes 786436
  1950.3 0.9 copy-start.50
  (26 other events, 18.8 us)
Sparse Core Ops, SparseCore 0:
  302.8 1295.3 all-reduce.4
where the time goes:
time: 1960 us
  waiting for transfers between devices  1290 us (66%)
  blocking collectives  544 us (28%)
  local copies, waits for them, and re-layouts  51.2 us (3%)
  matrix products  40.6 us (2%)
    unnamed x2, waiting for transfers between devices  1290 us
    psum x1, blocking collectives, body(): lax.psum((proj_part, biasw_part, chain_part, out_part), 'dap')  348 us
    all_gather x1, blocking collectives, body(): pair_bias = lax.all_gather(local_bias, 'dap', axis=1, tiled=True)  196 us
  transfers between devices with their start and end apart: 2, of which 1 were waited for; matrix products, arithmetic and copies ran while one was open for 2% of the time, Pallas kernels for 0%

commit v1 on v0

--- a/solution.py
+++ b/solution.py
@@ -88,7 +88,9 @@
         row_count, length, H
     )
     local_bias = jnp.transpose(local_bias, (2, 0, 1)).astype(jnp.bfloat16)
-    pair_bias = lax.all_gather(local_bias, "dap", axis=1, tiled=True)
+    pair_bias = jnp.concatenate(
+        lax.all_to_all(jnp.stack([local_bias] * lax.axis_size("dap")), "dap", 0, 0), axis=1
+    )
     same_chain = (chain_ids[:, None] == chain_ids[None, :]).astype(jnp.float32)
     masked = (token_mask.astype(jnp.float32) - 1.0) * 1000000000.0
     outputs = []

time: 1960 us -> 1820 us (0.929)
  blocking collectives: 544 us -> 348 us
  local copies, waits for them, and re-layouts: 51.2 us -> 77.5 us
    all_gather x1 -> x0, blocking collectives: 196 us -> none  [body(): pair_bias = lax.all_gather(local_bias, 'dap', axis=1, tiled=True)]
  transfers between devices with their start and end apart: 2 -> 3, of which waited for: 1 -> 2; matrix products, arithmetic and copies ran while one was open for 2% -> 3% of each run, Pallas kernels for 0% -> 0%
where the time goes in v1:
time: 1820 us; the launch traced here: 1810 us
  waiting for transfers between devices  1300 us (71%)
  blocking collectives  348 us (19%)
  local copies, waits for them, and re-layouts  77.5 us (4%)
  matrix products  45.6 us (3%)
  starting transfers between devices  21.3 us (1%)
    unnamed x2, waiting for transfers between devices  1290 us
    psum x1, blocking collectives, body(): lax.psum((proj_part, biasw_part, chain_part, out_part), 'dap')  348 us
  transfers between devices with their start and end apart: 3, of which 2 were waited for; matrix products, arithmetic and copies ran while one was open for 3% of the time, Pallas kernels for 0%

profile of v1, /device:TPU:32, one launch (start us, length us, event | category | flops | bytes accessed | tf_op | source)
XLA Modules:
  0.0 1814.9 jit_solution(2099227560655955000)
XLA Ops:
  7.2 1.1 convert_reduce_fusion
  9.6 1.1 stack.12
  10.6 14.9 all-to-all-start
  34.9 1.4 fusion.217
  36.3 10.2 all-to-all-done
  46.6 1.1 fusion.218
  47.6 1.0 squeeze.123
  49.5 7.0 while.115
  49.5 1.7 fusion.320
  53.0 1.7 fusion.320
  58.4 8.2 while.114
  59.0 1.8 fusion.316
  63.1 1.8 fusion.316
  68.5 8.1 while.113
  69.1 1.7 fusion.312
  73.1 1.7 fusion.312
  78.4 6.7 while.112
  79.0 1.8 fusion.308
  82.3 1.8 fusion.308
  85.9 2.2 multiply_convert_fusion
  89.1 0.8 fusion.178
  89.9 0.9 copy.91
  90.8 6.2 all-to-all-start.1
  97.3 0.9 fusion.219
  99.0 9.8 while.119
  99.0 1.4 fusion.365
  101.3 1.1 multiply_reduce_fusion.12
  103.8 1.4 fusion.365
  106.2 1.1 multiply_reduce_fusion.12
  110.5 10.7 while.118
  111.0 1.5 fusion.353
  112.6 1.1 multiply_reduce_fusion.11
  116.4 1.5 fusion.353
  118.0 1.1 multiply_reduce_fusion.11
  123.3 8.1 while.117
  123.3 1.4 fusion.341
  124.7 1.1 multiply_reduce_fusion.10
  127.3 1.4 fusion.341
  128.8 1.1 multiply_reduce_fusion.10
  133.3 12.9 while.116
  133.9 1.5 fusion.329
  140.3 1.5 fusion.329
  154.4 0.8 copy.133
  156.9 1.1 fusion.176
  158.0 2.0 pad_maximum_fusion
  167.7 1286.1 %all-reduce.5.cloned.1.call-done = (f32[4,256,256]{2,0,1:T(4,128)}, f32[128,512]{1,0:T(8,128)}, f32[128,128]{1,0:T(8,128)}) async-done(((f32[4,256,256]{2,0,1:T(4,128)}, f32[128,512]{1,0:T(8,128)}, f32[128,128]{1,0:T(8,128)}), (f32[4,256,256]{2,0,1:T(4,128)}, f32[128,512]{1,0:T(8,128)}, f32[128,128]{1,0:T(8,128)})) %all-reduce.5.cloned.1.call-update) | async-done | bytes 1376272
  1457.7 1.0 fusion.189
  1458.7 347.9 %all-reduce.1 = (f32[128,4]{0,1:T(4,128)}, f32[4]{0:T(128)}) all-reduce(f32[128,4]{0,1:T(4,128)S(1)} %fusion.180, f32[4]{0:T(128)S(1)} %broadcast_multiply_fusion.3), channel_id=1, replica_groups=mesh['dap'=128,'dp'=2] {'dap'}, use_global_device_ids=true, to_apply=%region_42.43 | all-reduce | flops 516 | bytes 4128 | tf_op jit(solution)/shard_map/psum | solution.py:181
  (363 shorter events, 86.8 us)
Async XLA Ops:
  7.2 27.3 %copy-start = (bf16[128,512]{1,0:T(8,128)(2,1)S(1)}, bf16[128,512]{1,0:T(8,128)(2,1)}, u32[]{:S(2)}) copy-start(bf16[128,512]{1,0:T(8,128)(2,1)} %param.27) | copy-start | bytes 393220
  7.2 1.1 copy-start.1
  10.6 35.9 %all-to-all-start = ((bf16[128,4,2,256]{3,2,1,0:T(2,128)(2,1)}), bf16[128,4,2,256]{3,2,1,0:T(2,128)(2,1)S(1)}, u32[]{:S(2)}, u32[]{:S(2)}) async-start(bf16[128,4,2,256]{3,2,1,0:T(2,128)(2,1)} %stack.12), calls=%async_computation | async-start | bytes 1048576 | tf_op jit(solution)/shard_map/all_to_all | solution.py:92
  48.6 0.9 copy-start.10
  48.6 1.0 copy-start.12
  51.3 0.9 copy-start.30
  54.7 0.9 copy-start.30
  57.4 0.9 copy-start.8
  57.4 1.0 copy-start.9
  60.7 0.9 copy-start.28
  64.8 0.9 copy-start.28
  67.6 0.9 copy-start.6
  67.6 1.0 copy-start.7
  70.8 0.9 copy-start.26
  74.8 0.9 copy-start.26
  77.5 0.9 copy-start.25
  88.2 0.9 copy-start.51
  90.8 76.1 %all-to-all-start.1 = ((f32[256,2,128]{2,1,0:T(2,128)}), f32[256,2,128]{2,1,0:T(2,128)S(1)}, u32[]{:S(2)}, u32[]{:S(2)}) async-start(f32[256,2,128]{2,1,0:T(2,128)} %copy.91), calls=%async_computation.1 | async-start | bytes 524288 | tf_op jit(solution)/shard_map/all_to_all | solution.py:116
  97.0 1356.7 %all-reduce.5.cloned.1.call-start = ((), (), s32[]{:S(2)}) async-start(), calls=%async_computation.2 | async-start | bytes 2752512
  97.2 0.9 copy-start.11
  97.2 1.0 copy-start.13
  97.3 1.1 copy-start.55
  100.4 0.9 copy-start.61
  102.9 0.9 copy-start.56
  105.3 0.9 copy-start.61
  107.8 0.9 copy-start.56
  108.7 0.9 copy-start.54
  109.6 0.9 copy-start.29
  109.6 0.9 copy-start.36
  109.6 0.9 copy-start.39
  114.0 0.9 copy-start.60
  119.4 0.9 copy-start.60
  121.2 1.3 copy-start.53
  121.8 0.9 copy-start.27
  126.2 0.9 copy-start.59
  130.2 0.9 copy-start.59
  131.3 1.3 copy-start.5
  131.3 1.3 copy-start.52
  131.9 1.0 copy-start.3
  135.4 0.9 copy-start.57
  138.0 0.9 copy-start.58
  141.9 0.9 copy-start.57
  144.5 0.9 copy-start.58
  154.4 1.0 copy-start.14
  154.4 1.0 copy-start.15
  156.9 1.1 copy-start.16
  156.9 1.1 copy-start.17
  1457.6 348.9 %copy-start.21 = (f32[128,512]{1,0:T(8,128)S(1)}, f32[128,512]{1,0:T(8,128)}, u32[]{:S(2)}) copy-start(f32[128,512]{1,0:T(8,128)} %get-tuple-element.2028) | copy-start | bytes 786436
  (57 other events, 40.5 us)
Sparse Core Ops, SparseCore 0:
  160.2 1293.5 all-reduce.4
